TPU v7x, 256 devices: a whole 4x4x8 slice. The times are simulated.
256 devices in a mesh: dp: 16 (over x, y_lo, core), fsdp: 16 (over z, y_hi).
Axes of the slice: x: 4, y: 4 (y_hi: 2, y_lo: 2; y = y_hi * 2 + y_lo), z: 8, core: 2. Of those that a mesh axis runs over, the one named last changes fastest.
Arguments:
- fields: bfloat16 [16, 6, 48, 48, 48, 128], P('dp', None, 'fsdp'), may hold values from -6 to 6
- targets: bfloat16 [16, 6, 48, 2304], P('dp', None, 'fsdp'), may hold values from -6 to 6
- lists: int32 [16, 6], P('dp'), may hold values from 0 to 5, each once within a row
- counts: int32 [16], replicated, may hold values from 1 to 6, as said below
- spectral_w: bfloat16 [32, 2, 128, 128], P('fsdp'), may hold values from -0.375 to 0.375
- local_w: bfloat16 [128, 128], replicated, may hold values from -0.5 to 0.5
- proj: float32 [128], replicated, may hold values from -0.5 to 0.5
Outputs:
- grad_spectral: float32 [32, 2, 128, 128], P('fsdp')
- grad_local: float32 [128, 128], replicated
Inputs may be any that keep to these rules, and one draw needn't show every extreme that they name: Each row of lists names every slot of its lane once; the first counts[l] entries of row l are lane l's live grids. `counts`: exactly one lane has 6 live grids; every other lane has 1 or 2.
All inputs are finite; a program needn't handle non-finite values.
Results may differ from a plain program's by a relative error of at most 0.0036.
The roundings to bfloat16 on the way count: a program that leaves them out, or rounds other values in their place, can miss the bound.
Values may be sent and summed in bfloat16 or wider, within the bound.
A program may use at most 64 MiB of HBM per device.

v0:
```python
import functools
import math

import jax
import jax.numpy as jnp
import numpy as np
from jax import lax
from jax.experimental import pallas as pl
from jax.experimental.pallas import tpu as pltpu
from jax.sharding import PartitionSpec as P

MX, MY, MZ = 4, 4, 2
N_DEV = 16
ROWS = MY * MZ * 2
ROOT_HALF = 0.7071067811865476
INV_ROOT_TWO_PI = 0.3989422804014327
LOG2_E = 1.4426950408889634
MESH = pl.DeviceIdType.MESH
PART = 1152
UNROLL = 3
INPUTS = 9
SHARED = 2


def phases(ids, length):
    product = (ids[:, None] * np.arange(length)[None, :]) % length
    angle = product.astype(np.float32) * np.float32(2.0 * math.pi / length)
    return np.cos(angle).astype(np.float32), np.sin(angle).astype(np.float32)


def split_bf16(values):
    high = values.astype(jnp.bfloat16)
    low = (values - high.astype(np.float32)).astype(jnp.bfloat16)
    return high, low


@functools.lru_cache(maxsize=None)
def tables(length):
    cos_x, sin_x = phases(np.arange(MX) - MX // 2, length)
    cos_y, sin_y = phases(np.arange(MY) - MY // 2, length)
    cos_z, sin_z = phases(np.arange(MZ), length)
    round_z = lambda t: t.astype(jnp.bfloat16).astype(np.float32)

    def product(cz, sz):
        re = cos_y[:, None, :, None] * cz[None, :, None, :] - sin_y[:, None, :, None] * sz[None, :, None, :]
        im = sin_y[:, None, :, None] * cz[None, :, None, :] + cos_y[:, None, :, None] * sz[None, :, None, :]
        shape = (MY, MZ, length * length)
        return re.reshape(shape), -im.reshape(shape)

    re, im = product(round_z(cos_z), round_z(sin_z))
    forward = np.concatenate(split_bf16(np.stack([re, im], axis=2).reshape(ROWS, -1)), axis=0)
    re, im = product(cos_z, sin_z)
    back = np.stack([re, im], axis=2).reshape(ROWS, -1) * np.float32(float(MX * MY * MZ) ** -0.5)
    high, low = split_bf16(back)
    inverse = np.concatenate([high, low, high], axis=0)
    return np.stack([cos_x, sin_x]).reshape(2, -1), forward, inverse


def times_i(values):
    rows, width = values.shape
    grouped = values.reshape(rows // 8, 8, width)
    even = lax.broadcasted_iota(jnp.int32, grouped.shape, 1) % 2 == 0
    turned = jnp.where(even, -pltpu.roll(grouped, 7, 1), pltpu.roll(grouped, 1, 1))
    return turned.reshape(rows, width)


def dot(a, b):
    return jnp.dot(a, b, preferred_element_type=jnp.float32)


def kernel(
    length, slots, planes,
    fields, *rest,
):
    inputs, (out_spec, out_local), rest = rest[:INPUTS], rest[INPUTS : INPUTS + 2], rest[INPUTS + 2 :]
    kept, rest = rest[:INPUTS], rest[INPUTS:]
    fwd_table, xphase, lists, counts, targets, inv_table, local_w, proj, spec_w = kept
    (
    fbuf, pbuf, p_turned, f_share, d_buf, cell_table, rhs, inv_rows, inv_share, tgt, tgt_send, tgt_share, acc, local_acc,
    ca_send, ca_recv, cb_send, cb_recv, sa_send, sa_recv, sb_send, sb_recv, cg_send, cg_recv,
    ba_send, ba_recv, bb_send, bb_recv, bg_send, bg_recv,
    l_recv, m_send, m_recv, n_send, n_recv,
    load_sem, send_sem, recv_sem, share_send_sem, share_recv_sem,
    ) = rest
    cells = length * length
    width = fields.shape[-1]
    near = slots - 2 * SHARED
    work = slots - SHARED
    units = work * planes
    half = units // 2
    parts = cells // PART
    me = {"fsdp": lax.axis_index("fsdp"), "dp": lax.axis_index("dp")}
    partner = me["dp"] + 1 - 2 * lax.rem(me["dp"], 2)
    offsets = [8 + ((t + 1) // 2) * (1 - 2 * (t % 2)) for t in range(N_DEV - 1)]

    def peer_of(axis, t):
        return lax.rem(me[axis] + offsets[t], N_DEV)

    exchanges = {
        0: ("fsdp", lambda peer: ca_send.at[peer], ca_recv),
        1: ("fsdp", lambda peer: sa_send, sa_recv),
        2: ("dp", lambda peer: cg_send, cg_recv),
        3: ("fsdp", lambda peer: ba_send.at[peer], ba_recv),
        4: ("dp", lambda peer: local_acc.at[peer], l_recv),
        5: ("dp", lambda peer: bg_send, bg_recv),
        6: ("fsdp", lambda peer: m_send, m_recv),
        7: ("dp", lambda peer: n_send, n_recv),
        8: ("fsdp", lambda peer: cb_send.at[peer], cb_recv),
        9: ("fsdp", lambda peer: sb_send, sb_recv),
        10: ("fsdp", lambda peer: bb_send.at[peer], bb_recv),
    }

    def start(phase):
        axis, src, landing = exchanges[phase]
        for t in range(N_DEV - 1):
            peer = peer_of(axis, t)
            pltpu.make_async_remote_copy(
                src_ref=src(peer), dst_ref=landing.at[me[axis]],
                send_sem=send_sem.at[phase], recv_sem=recv_sem.at[phase],
                device_id={axis: peer}, device_id_type=MESH,
            ).start()

    def all_of(phase):
        axis, _, landing = exchanges[phase]
        bytes_of_all = landing.at[pl.ds(0, N_DEV - 1)]
        return pltpu.make_async_remote_copy(
            src_ref=bytes_of_all, dst_ref=bytes_of_all,
            send_sem=send_sem.at[phase], recv_sem=recv_sem.at[phase],
            device_id={axis: peer_of(axis, 0)}, device_id_type=MESH,
        )

    wait_recv = lambda phase: all_of(phase).wait_recv()
    wait_send = lambda phase: all_of(phase).wait_send()

    def share(index, src, dst):
        return pltpu.make_async_remote_copy(
            src_ref=src, dst_ref=dst,
            send_sem=share_send_sem.at[index], recv_sem=share_recv_sem.at[index],
            device_id={"dp": partner}, device_id_type=MESH,
        )

    shares = [
        share(0, tgt_send, tgt_share),
        share(1, pbuf.at[pl.ds(work, SHARED)], f_share),
        share(2, inv_rows.at[pl.ds(units, SHARED * planes)], inv_share),
    ]

    def load(slot):
        return pltpu.make_async_copy(fields.at[slot], fbuf.at[slot], load_sem.at[slot])

    fetches = [
        pltpu.make_async_copy(src, dst, load_sem.at[slots + index]) for index, (src, dst) in enumerate(zip(inputs, kept))
    ]
    for fetch in fetches[:4]:
        fetch.start()
    for slot in range(slots):
        load(slot).start()
    for fetch in fetches[4:]:
        fetch.start()

    barrier = pltpu.get_barrier_semaphore()
    for axis in ("fsdp", "dp"):
        for t in range(N_DEV - 1):
            pl.semaphore_signal(barrier, inc=1, device_id={axis: peer_of(axis, t)}, device_id_type=MESH)

    def x_phase(part_index, k1, plane):
        return xphase[part_index, k1 * length + me["fsdp"] * planes + plane]

    def fold_modes(slot, plane, product):
        direct = product[0:ROWS] + product[ROWS : 2 * ROWS]
        turned = times_i(direct)
        for k1 in range(MX):
            acc[slot, k1] += x_phase(0, k1, plane) * direct - x_phase(1, k1, plane) * turned

    def pack_modes(send, picks):
        for k1 in range(MX):
            for k2 in range(MY):
                send[k1 * MY + k2] = jnp.concatenate([acc[p, k1, 4 * k2 : 4 * k2 + 4] for p in picks], axis=0)

    acc[...] = jnp.zeros_like(acc)
    for fetch in fetches[:4]:
        fetch.wait()
    order = [lists[0, j] for j in range(slots)]
    my_count, partner_count = counts[me["dp"]], counts[partner]
    mine = my_count > 2
    shared_live = jnp.maximum(my_count, partner_count) > 2

    for slot in range(slots):
        load(slot).wait()

        for plane in range(planes):
            fold_modes(slot, plane, dot(fwd_table[...], fbuf[slot, plane]))
    pack_modes(ca_send, order[:near])
    pl.semaphore_wait(barrier, 2 * (N_DEV - 1))
    start(0)
    pack_modes(cb_send, order[near:])

    for fetch in fetches[4:]:
        fetch.wait()
    tgt[...] = jnp.zeros_like(tgt)
    tgt_send[...] = jnp.zeros_like(tgt_send)
    for j in range(SHARED):
        tgt_send[planes * j : planes * (j + 1)] = targets[order[work + j]].astype(jnp.float32)
    shares[0].start()

    def by_position(j):
        def one(plane, carry):
            value = fbuf[order[j], plane]
            pbuf[j, plane] = value
            if j < near:
                p_turned[j, plane] = value.T
            return carry

        lax.fori_loop(0, planes, one, 0)

    for j in range(work, slots):
        by_position(j)
    shares[1].start()
    ca_recv[me["fsdp"]] = ca_send[me["fsdp"]]
    cb_recv[me["fsdp"]] = cb_send[me["fsdp"]]
    start(8)
    for j in range(work):
        tgt[planes * j : planes * (j + 1)] = targets[order[j]].astype(jnp.float32)
        by_position(j)
    rhs[...] = jnp.zeros_like(rhs)
    rhs[0:width, 0:width] = local_w[...]
    acc[...] = jnp.zeros_like(acc)
    local_acc[...] = jnp.zeros_like(local_acc)
    d_buf[...] = jnp.zeros_like(d_buf)
    grid_total = counts[0]
    for lane in range(1, N_DEV):
        grid_total = grid_total + counts[lane]
    scale = 1.0 / (jnp.zeros((1, width), jnp.float32) + grid_total.astype(jnp.float32))
    shares[0].wait_recv()
    tgt[half : 2 * half] = jnp.where(mine, tgt[half : 2 * half], tgt_share[0:half])
    cell_rows = jnp.concatenate(
        [inv_table[...], tgt[...].astype(jnp.bfloat16), jnp.zeros((width - 3 * ROWS - 16, cells), jnp.bfloat16)], axis=0
    )
    cell_table[...] = cell_rows.T

    def sum_of(ref):
        value = ref[0]
        for peer in range(1, N_DEV):
            value = value + ref[peer]
        return value

    def mix(landing, send):
        coeff = (sum_of(landing) * float(length) ** -1.5).astype(jnp.bfloat16)
        coeff_f = coeff.astype(jnp.float32)
        turned = times_i(coeff_f).astype(jnp.bfloat16)
        third = (lax.broadcasted_iota(jnp.int32, coeff.shape, 0) // 2) % 2
        mixed = [dot(coeff, spec_w[k3, 0]) + dot(turned, spec_w[k3, 1]) for k3 in range(MZ)]
        send[...] = jnp.where(third == 0, mixed[0], mixed[1]).astype(jnp.bfloat16)
        return coeff_f

    wait_recv(0)
    coeff_near = mix(ca_recv, sa_send)
    start(1)
    wait_recv(8)
    coeff_far = mix(cb_recv, sb_send)
    start(9)
    cg_send[...] = jnp.concatenate([coeff_near, coeff_far], axis=0)
    sa_recv[me["fsdp"]] = sa_send[...]
    sb_recv[me["fsdp"]] = sb_send[...]
    cg_recv[me["dp"]] = cg_send[...]

    def inverse_rows(landing, first, last):
        for k1 in range(MX):
            owners = [landing[k1 * MY + k2].astype(jnp.float32) for k2 in range(MY)]
            for j in range(last - first):
                piece = jnp.concatenate([o[4 * j : 4 * j + 4] for o in owners], axis=0)
                turned_piece = times_i(piece)
                for plane in range(planes):
                    term = x_phase(0, k1, plane) * piece + x_phase(1, k1, plane) * turned_piece
                    unit = (first + j) * planes + plane
                    if k1 == 0:
                        inv_rows[unit] = term
                    else:
                        inv_rows[unit] += term

    shares[1].wait_recv()

    def choose(k, carry):
        slot, plane = near + k // planes, k % planes
        value = jnp.where(mine, pbuf[slot, plane], f_share[k // planes, plane])
        pbuf[slot, plane] = value
        p_turned[slot, plane] = value.T
        return carry

    lax.fori_loop(0, half, choose, 0)
    wait_recv(1)
    inverse_rows(sa_recv, 0, near)

    picks = lax.broadcasted_iota(jnp.int32, (width, width), 0)

    def reduce_part(unit, part_index):
        slot, plane = unit // planes, unit % planes
        rows_here = pl.ds(part_index * PART, PART)
        left = jnp.concatenate([p_turned[slot, plane, :, rows_here], fwd_table[:, rows_here]], axis=0)
        product = dot(left, d_buf[part_index])
        local_acc[...] += product[0:width, 0:width].reshape(local_acc.shape)
        fold_modes(slot, plane, product[width:, 0:width])

    def point(unit):
        slot, plane = unit // planes, unit % planes
        live = jnp.where(slot < near, jnp.where(slot < my_count, 1, 0), jnp.where(shared_live, 1, 0))
        weight = proj[...] * scale * live.astype(jnp.float32)
        half_proj, half_weight, bell_weight = 0.5 * proj[...], 0.5 * weight, INV_ROOT_TWO_PI * weight
        values = inv_rows[unit]
        high = values.astype(jnp.bfloat16)
        low = (values - high.astype(jnp.float32)).astype(jnp.bfloat16)
        rhs[width : width + 3 * ROWS, 0:width] = jnp.concatenate([high, high, low], axis=0)
        rhs[width : 2 * width, width : 2 * width] = jnp.where(picks == 3 * ROWS + unit, 1.0, 0.0).astype(jnp.bfloat16)
        for part_index in range(parts):
            rows_here = pl.ds(part_index * PART, PART)
            left = jnp.concatenate([pbuf[slot, plane, rows_here], cell_table[rows_here]], axis=1)
            both = dot(left, rhs[...])
            pre, target = both[:, 0:width], both[:, width : 2 * width]
            gate = lax.erf(pre * ROOT_HALF) + 1.0
            bell = jnp.exp2(pre * pre * (-0.5 * LOG2_E))
            pred = jnp.sum(pre * gate * half_proj, axis=1, keepdims=True)
            slope = gate * half_weight + pre * bell * bell_weight
            d_buf[part_index, :, 0:width] = ((pred - target) * slope).astype(jnp.bfloat16)
            if part_index == 0:
                reduce_part(jnp.maximum(unit - 1, 0), parts - 1)
            else:
                reduce_part(unit, part_index - 1)

    def step(index, carry):
        first = index * UNROLL

        @pl.when(first == planes)
        def _():
            wait_recv(9)
            inverse_rows(sb_recv, near, slots)
            shares[2].start()
            start(2)

        @pl.when(first == half)
        def _():
            shares[2].wait_recv()
            inv_rows[half:units] = jnp.where(mine, inv_rows[half:units], inv_share[0:half])

        @pl.when(first == half + planes)
        def _():
            pack_modes(ba_send, range(near))
            start(3)
            ba_recv[me["fsdp"]] = ba_send[me["fsdp"]]

        for sub in range(UNROLL):
            point(first + sub)
        return carry

    lax.fori_loop(0, units // UNROLL, step, 0)
    reduce_part(units - 1, parts - 1)

    start(4)
    pack_modes(bb_send, range(near, work))
    start(10)
    l_recv[me["dp"]] = local_acc[me["dp"]]
    bb_recv[me["fsdp"]] = bb_send[me["fsdp"]]
    back_scale = float(MX * MY * MZ) ** -0.5
    wait_recv(3)
    near_value = sum_of(ba_recv) * back_scale

    wait_recv(4)
    m_value = sum_of(l_recv)
    m_send[...] = m_value
    start(6)
    m_recv[me["fsdp"]] = m_value
    wait_recv(10)
    bg_send[...] = jnp.concatenate([near_value, sum_of(bb_recv) * back_scale], axis=0)
    start(5)
    bg_recv[me["dp"]] = bg_send[...]

    wait_recv(2)
    first, far = 4 * near, 4 * work
    pieces = []
    for lane in range(N_DEV):
        taken = jnp.where(counts[lane] > 2, cg_recv[lane, first:far], cg_recv[lane ^ 1, far : 4 * slots])
        pieces += [cg_recv[lane, 0:first], taken]
    coeff_all = jnp.concatenate(pieces, axis=0)
    every = N_DEV * far
    third = (lax.broadcasted_iota(jnp.int32, (every, width), 0) // 2) % 2
    left = jnp.concatenate([jnp.where(third == k3, coeff_all, 0.0) for k3 in range(MZ)], axis=1)
    left = left.astype(jnp.bfloat16).T

    wait_recv(6)
    n_value = sum_of(m_recv)
    n_send[...] = n_value
    start(7)
    n_recv[me["dp"]] = n_value

    wait_recv(5)
    back_all = bg_recv[...].reshape(every, width)
    right = jnp.concatenate([back_all, -times_i(back_all)], axis=1)
    right_high = right.astype(jnp.bfloat16)
    right_low = (right - right_high.astype(jnp.float32)).astype(jnp.bfloat16)
    grad = dot(left, right_high) + dot(left, right_low)
    for k3 in range(MZ):
        for part_index in range(2):
            out_spec[k3, part_index] = grad[
                k3 * width : (k3 + 1) * width, part_index * width : (part_index + 1) * width
            ]

    wait_recv(7)
    out_local[...] = n_recv[...].reshape(width, width)
    for phase in exchanges:
        wait_send(phase)
    for one in shares:
        one.wait_send()


def copy_out(spec_in, local_in, out_spec, out_local, sem):
    copies = [
        pltpu.make_async_copy(src, dst, sem.at[index])
        for index, (src, dst) in enumerate(((spec_in, out_spec), (local_in, out_local)))
    ]
    for copy in copies:
        copy.start()
    for copy in copies:
        copy.wait()


def body(fields, targets, lists, counts, spectral_w, local_w, proj):
    _, slots, planes, length, _, width = fields.shape
    cells = length * length
    work, near = slots - SHARED, slots - 2 * SHARED
    xphase, fwd_table, inv_table = tables(length)
    vmem = pl.BlockSpec(memory_space=pltpu.VMEM)
    f32, bf16 = jnp.float32, jnp.bfloat16
    results = (
        jax.ShapeDtypeStruct(spectral_w.shape, f32),
        jax.ShapeDtypeStruct(local_w.shape, f32),
    )
    fixed = (
        jnp.asarray(fwd_table), jnp.asarray(xphase), lists, counts, targets.reshape(slots, planes, cells),
        jnp.asarray(inv_table), local_w, proj.reshape(1, width), spectral_w,
    )
    in_smem = (1, 2, 3)
    eight = pltpu.VMEM((N_DEV, 8, width), f32)
    sixteen = pltpu.VMEM((N_DEV, 4 * (slots - near), width), f32)
    hbm = pl.BlockSpec(memory_space=pltpu.HBM)
    grads = pl.pallas_call(
        functools.partial(kernel, length, slots, planes),
        out_shape=tuple(pltpu.VMEM(r.shape, r.dtype) for r in results),
        in_specs=[hbm] * (1 + INPUTS),
        out_specs=(vmem, vmem),
        scratch_shapes=[
            *((pltpu.SMEM if index in in_smem else pltpu.VMEM)(a.shape, a.dtype) for index, a in enumerate(fixed)),
            pltpu.VMEM((slots, planes, cells, width), bf16),
            pltpu.VMEM((slots, planes, cells, width), bf16),
            pltpu.VMEM((work, planes, width, cells), bf16),
            pltpu.VMEM((SHARED, planes, cells, width), bf16),
            pltpu.VMEM((cells // PART, PART, 2 * width), bf16),
            pltpu.VMEM((cells, width), bf16),
            pltpu.VMEM((2 * width, 2 * width), bf16),
            pltpu.VMEM((slots * planes, ROWS, width), f32),
            pltpu.VMEM((SHARED * planes, ROWS, width), f32),
            pltpu.VMEM((16, cells), f32), pltpu.VMEM((8, cells), f32), pltpu.VMEM((8, cells), f32),
            pltpu.VMEM((slots, MX, ROWS, width), f32),
            pltpu.VMEM((N_DEV, width // N_DEV, width), f32),
            eight, eight, sixteen, sixteen,
            pltpu.VMEM((8, width), bf16), pltpu.VMEM((N_DEV, 8, width), bf16),
            pltpu.VMEM((16, width), bf16), pltpu.VMEM((N_DEV, 16, width), bf16),
            pltpu.VMEM((4 * slots, width), f32), pltpu.VMEM((N_DEV, 4 * slots, width), f32),
            eight, eight, eight, eight,
            pltpu.VMEM((4 * work, width), f32), pltpu.VMEM((N_DEV, 4 * work, width), f32),
            eight,
            pltpu.VMEM((8, width), f32), eight,
            pltpu.VMEM((8, width), f32), eight,
            pltpu.SemaphoreType.DMA((slots + INPUTS,)),
            pltpu.SemaphoreType.DMA((11,)),
            pltpu.SemaphoreType.DMA((11,)),
            pltpu.SemaphoreType.DMA((3,)),
            pltpu.SemaphoreType.DMA((3,)),
        ],
        compiler_params=pltpu.CompilerParams(
            collective_id=0, has_side_effects=True, vmem_limit_bytes=48 * 1024 * 1024,

        ),
        name="fno_step",
    )(*(pltpu.with_memory_space_constraint(a, pltpu.HBM) for a in (fields.reshape(slots, planes, cells, width), *fixed)))
    return pl.pallas_call(
        copy_out, out_shape=results, in_specs=[vmem, vmem], out_specs=(hbm, hbm), name="copy_out",
        scratch_shapes=[pltpu.SemaphoreType.DMA((2,))],
        compiler_params=pltpu.CompilerParams(vmem_limit_bytes=2 * 1024 * 1024),
    )(*grads)


def solution(mesh):
    return jax.shard_map(
        body,
        mesh=mesh,
        in_specs=(
            P("dp", None, "fsdp", None, None, None),
            P("dp", None, "fsdp", None),
            P("dp", None),
            P(),
            P("fsdp", None, None, None),
            P(),
            P(),
        ),
        out_specs=(P("fsdp", None, None, None), P()),
        check_vma=False,
    )
```

profile of v0, /device:TPU:1, one launch (start us, length us, event | category | flops | bytes accessed | tf_op | source)
XLA Modules:
  0.0 50.3 jit_solution(16027054333890041982)
XLA Ops:
  0.6 49.0 %fno_step.1 = (f32[2,2,128,128]{3,2,1,0:T(8,128)S(1)}, f32[128,128]{1,0:T(8,128)S(1)}) custom-call(bf16[6,3,2304,128]{3,2,1,0:T(8,128)(2,1)} %bitcast.3, bf16[32,2304]{1,0:T(8,128)(2,1)} %constant.6.clone.rest_0_, f32[2,192]{1,0:T(2,128)} %constant.7.clone.rest_1_, s32[1,6]{1,0:T(1,128)} %rest_2_.1, s32[16]{0:T(128)} %rest_3_.1, ...), custom_call_target="tpu_custom_call" | custom-call | tf_op jit(solution)/shard_map/fno_step/pallas_call | solution.py:444
  49.6 0.7 %copy_out.1 = (f32[2,2,128,128]{3,2,1,0:T(8,128)}, f32[128,128]{1,0:T(8,128)}) custom-call(f32[2,2,128,128]{3,2,1,0:T(8,128)S(1)} %get-tuple-element.4.spec_in, f32[128,128]{1,0:T(8,128)S(1)} %get-tuple-element.5.local_in), custom_call_target="tpu_custom_call" | custom-call | tf_op jit(solution)/shard_map/copy_out/pallas_call | solution.py:484
where the time goes:
time: 50.4 us; the launch traced here: 50.3 us
  Pallas kernels  49.7 us (99%)
  between operations  0.64 us (1%)
    pallas_call x1, Pallas kernels, body(): pl.pallas_call(functools.partial(kernel, length, slots, planes), out_shap...  49 us

commit v1 on v0

--- a/solution.py
+++ b/solution.py
@@ -76,7 +76,7 @@
     kept, rest = rest[:INPUTS], rest[INPUTS:]
     fwd_table, xphase, lists, counts, targets, inv_table, local_w, proj, spec_w = kept
     (
-    fbuf, pbuf, p_turned, f_share, d_buf, cell_table, rhs, inv_rows, inv_share, tgt, tgt_send, tgt_share, acc, local_acc,
+    fbuf, pbuf, p_turned, f_share, d_buf, cell_table, rhs, back_part, inv_rows, inv_share, tgt, tgt_send, tgt_share, acc, local_acc,
     ca_send, ca_recv, cb_send, cb_recv, sa_send, sa_recv, sb_send, sb_recv, cg_send, cg_recv,
     ba_send, ba_recv, bb_send, bb_recv, bg_send, bg_recv,
     l_recv, m_send, m_recv, n_send, n_recv,
@@ -222,19 +222,40 @@
     for j in range(work):
         tgt[planes * j : planes * (j + 1)] = targets[order[j]].astype(jnp.float32)
         by_position(j)
-    rhs[...] = jnp.zeros_like(rhs)
-    rhs[0:width, 0:width] = local_w[...]
-    acc[...] = jnp.zeros_like(acc)
-    local_acc[...] = jnp.zeros_like(local_acc)
-    d_buf[...] = jnp.zeros_like(d_buf)
     grid_total = counts[0]
     for lane in range(1, N_DEV):
         grid_total = grid_total + counts[lane]
     scale = 1.0 / (jnp.zeros((1, width), jnp.float32) + grid_total.astype(jnp.float32))
+    root_scale = jnp.sqrt(scale)
+
+    def root_of(unit):
+        slot = unit // planes
+        live = jnp.where(slot < near, jnp.where(slot < my_count, 1, 0), jnp.where(shared_live, 1, 0))
+        return root_scale * live.astype(jnp.float32)
+
+    picks = lax.broadcasted_iota(jnp.int32, (width, width), 0)
+
+    def clear_rhs(unit, carry):
+        rhs[unit] = jnp.zeros((2 * width, 2 * width), jnp.bfloat16)
+        rhs[unit, 0:width, 0:width] = local_w[...]
+        left_over = root_of(unit)
+        block = jnp.zeros((width, width), jnp.bfloat16)
+        for copy in range(3):
+            piece = left_over.astype(jnp.bfloat16).astype(jnp.float32)
+            block = block + jnp.where(picks == 3 * ROWS + 16 * copy + unit, piece, 0.0).astype(jnp.bfloat16)
+            left_over = left_over - piece
+        rhs[unit, width : 2 * width, width : 2 * width] = block
+        return carry
+
+    lax.fori_loop(0, units, clear_rhs, 0)
+    back_part[...] = jnp.zeros_like(back_part)
+    acc[...] = jnp.zeros_like(acc)
+    local_acc[...] = jnp.zeros_like(local_acc)
+    d_buf[...] = jnp.zeros_like(d_buf)
     shares[0].wait_recv()
     tgt[half : 2 * half] = jnp.where(mine, tgt[half : 2 * half], tgt_share[0:half])
     cell_rows = jnp.concatenate(
-        [inv_table[...], tgt[...].astype(jnp.bfloat16), jnp.zeros((width - 3 * ROWS - 16, cells), jnp.bfloat16)], axis=0
+        [inv_table[...]] + [tgt[...].astype(jnp.bfloat16)] * 3 + [jnp.zeros((width - 3 * ROWS - 48, cells), jnp.bfloat16)], axis=0
     )
     cell_table[...] = cell_rows.T
 
@@ -278,6 +299,7 @@
                     else:
                         inv_rows[unit] += term
 
+    start(2)
     shares[1].wait_recv()
 
     def choose(k, carry):
@@ -291,7 +313,14 @@
     wait_recv(1)
     inverse_rows(sa_recv, 0, near)
 
-    picks = lax.broadcasted_iota(jnp.int32, (width, width), 0)
+    def set_rhs(first, last):
+        for unit in range(first, last):
+            values = inv_rows[unit]
+            high = values.astype(jnp.bfloat16)
+            low = (values - high.astype(jnp.float32)).astype(jnp.bfloat16)
+            rhs[unit, width : width + 3 * ROWS, 0:width] = jnp.concatenate([high, high, low], axis=0)
+
+    set_rhs(0, half)
 
     def reduce_part(unit, part_index):
         slot, plane = unit // planes, unit % planes
@@ -299,27 +328,25 @@
         left = jnp.concatenate([p_turned[slot, plane, :, rows_here], fwd_table[:, rows_here]], axis=0)
         product = dot(left, d_buf[part_index])
         local_acc[...] += product[0:width, 0:width].reshape(local_acc.shape)
-        fold_modes(slot, plane, product[width:, 0:width])
+        if part_index == parts - 1:
+            fold_modes(slot, plane, back_part[...] + product[width:, 0:width])
+        else:
+            back_part[...] = product[width:, 0:width]
 
     def point(unit):
         slot, plane = unit // planes, unit % planes
-        live = jnp.where(slot < near, jnp.where(slot < my_count, 1, 0), jnp.where(shared_live, 1, 0))
-        weight = proj[...] * scale * live.astype(jnp.float32)
-        half_proj, half_weight, bell_weight = 0.5 * proj[...], 0.5 * weight, INV_ROOT_TWO_PI * weight
-        values = inv_rows[unit]
-        high = values.astype(jnp.bfloat16)
-        low = (values - high.astype(jnp.float32)).astype(jnp.bfloat16)
-        rhs[width : width + 3 * ROWS, 0:width] = jnp.concatenate([high, high, low], axis=0)
-        rhs[width : 2 * width, width : 2 * width] = jnp.where(picks == 3 * ROWS + unit, 1.0, 0.0).astype(jnp.bfloat16)
+        root_proj = 0.5 * proj[...] * root_of(unit)
+        bell_proj = 2.0 * INV_ROOT_TWO_PI * root_proj
         for part_index in range(parts):
             rows_here = pl.ds(part_index * PART, PART)
             left = jnp.concatenate([pbuf[slot, plane, rows_here], cell_table[rows_here]], axis=1)
-            both = dot(left, rhs[...])
+            both = dot(left, rhs[unit])
             pre, target = both[:, 0:width], both[:, width : 2 * width]
             gate = lax.erf(pre * ROOT_HALF) + 1.0
             bell = jnp.exp2(pre * pre * (-0.5 * LOG2_E))
-            pred = jnp.sum(pre * gate * half_proj, axis=1, keepdims=True)
-            slope = gate * half_weight + pre * bell * bell_weight
+            active = gate * root_proj
+            pred = jnp.sum(pre * active, axis=1, keepdims=True)
+            slope = active + pre * bell * bell_proj
             d_buf[part_index, :, 0:width] = ((pred - target) * slope).astype(jnp.bfloat16)
             if part_index == 0:
                 reduce_part(jnp.maximum(unit - 1, 0), parts - 1)
@@ -334,12 +361,12 @@
             wait_recv(9)
             inverse_rows(sb_recv, near, slots)
             shares[2].start()
-            start(2)
 
         @pl.when(first == half)
         def _():
             shares[2].wait_recv()
             inv_rows[half:units] = jnp.where(mine, inv_rows[half:units], inv_share[0:half])
+            set_rhs(half, units)
 
         @pl.when(first == half + planes)
         def _():
@@ -454,7 +481,8 @@
             pltpu.VMEM((SHARED, planes, cells, width), bf16),
             pltpu.VMEM((cells // PART, PART, 2 * width), bf16),
             pltpu.VMEM((cells, width), bf16),
-            pltpu.VMEM((2 * width, 2 * width), bf16),
+            pltpu.VMEM((work * planes, 2 * width, 2 * width), bf16),
+            pltpu.VMEM((2 * ROWS, width), f32),
             pltpu.VMEM((slots * planes, ROWS, width), f32),
             pltpu.VMEM((SHARED * planes, ROWS, width), f32),
             pltpu.VMEM((16, cells), f32), pltpu.VMEM((8, cells), f32), pltpu.VMEM((8, cells), f32),

time: 50.4 us -> 49.3 us (0.978)
  Pallas kernels: 49.7 us -> 48.6 us
    pallas_call x1, Pallas kernels: 49 us -> 47.9 us  [body(): pl.pallas_call(functools.partial(kernel, length, slots, planes), out_shap...]
where the time goes in v1:
time: 49.3 us
  Pallas kernels  48.6 us (99%)
  between operations  0.64 us (1%)
    pallas_call x1, Pallas kernels, body(): pl.pallas_call(functools.partial(kernel, length, slots, planes), out_shap...  47.9 us

profile of v1, /device:TPU:1, one launch (start us, length us, event | category | flops | bytes accessed | tf_op | source)
XLA Modules:
  0.0 49.3 jit_solution(16764219762017091639)
XLA Ops:
  0.6 47.9 %fno_step.1 = (f32[2,2,128,128]{3,2,1,0:T(8,128)S(1)}, f32[128,128]{1,0:T(8,128)S(1)}) custom-call(bf16[6,3,2304,128]{3,2,1,0:T(8,128)(2,1)} %bitcast.3, bf16[32,2304]{1,0:T(8,128)(2,1)} %constant.6.clone.rest_0_, f32[2,192]{1,0:T(2,128)} %constant.7.clone.rest_1_, s32[1,6]{1,0:T(1,128)} %rest_2_.1, s32[16]{0:T(128)} %rest_3_.1, ...), custom_call_target="tpu_custom_call" | custom-call | tf_op jit(solution)/shard_map/fno_step/pallas_call | solution.py:471
  48.5 0.7 %copy_out.1 = (f32[2,2,128,128]{3,2,1,0:T(8,128)}, f32[128,128]{1,0:T(8,128)}) custom-call(f32[2,2,128,128]{3,2,1,0:T(8,128)S(1)} %get-tuple-element.4.spec_in, f32[128,128]{1,0:T(8,128)S(1)} %get-tuple-element.5.local_in), custom_call_target="tpu_custom_call" | custom-call | tf_op jit(solution)/shard_map/copy_out/pallas_call | solution.py:512
